TPU v7x, 32 devices: a whole 2x2x4 slice. The times are simulated.
32 devices in a mesh: groups: 2 (over y), rows: 4 (over z), feat: 4 (over x, core).
Axes of the slice: x: 2, y: 2, z: 4, core: 2. Of those that a mesh axis runs over, the one named last changes fastest.
Arguments:
- student: float32 [1280, 4096], P(('groups', 'rows'), 'feat'), parts along dimension 0, may hold values from -1 to 1
- teacher: bfloat16 [1280, 1024], P(('groups', 'rows'), 'feat'), parts along dimension 0, may hold values from -1 to 1
Outputs:
- row_loss: float32 [1280], P(('groups', 'rows')), parts along dimension 0
- student_grad: float32 [1280, 4096], P(('groups', 'rows'), 'feat'), parts along dimension 0
There are 2 independent parts, one for each index of `groups`. A program takes and returns all parts, laid end to end along the dimension named above; each array names one. Nothing has to cross between parts.
All inputs are finite; a program needn't handle non-finite values.
Results may differ from a plain program's by a relative error of at most 0.0085.
Values may be sent and summed in bfloat16 or wider, within the bound.
A program may use at most 64 MiB of HBM per device.

v0:
```python
import jax
import jax.numpy as jnp
from jax import lax
from jax.sharding import PartitionSpec as P

D = 4096
EPSILON = 1e-06


def shifted(block, axis, distance):
    devices = range(lax.axis_size(axis))
    route = [((i - distance) % len(devices), i) for i in devices]
    return lax.ppermute(block, axis, route)


def on_device(student, teacher):
    cycle = lax.axis_size("rows")
    rows_here = student.shape[0]
    width = student.shape[1]
    embeds = rows_here * cycle
    squares = lax.psum(jnp.sum(student * student, axis=1), "feat")
    scaling = lax.rsqrt(squares + EPSILON)
    unit = student * scaling[:, None]
    unit_half = unit.astype(jnp.bfloat16)
    packed = jnp.concatenate([unit_half, teacher], axis=1)
    contract = (((1,), (1,)), ((), ()))

    def absorb(carry, visitor):
        losses, pulled = carry
        other_unit = visitor[:, :width]
        other_teacher = visitor[:, width:]
        student_term = lax.dot_general(
            unit_half, other_unit, contract, preferred_element_type=jnp.float32
        )
        teacher_term = lax.dot_general(
            teacher, other_teacher, contract, preferred_element_type=jnp.float32
        )
        differ = lax.psum((student_term - teacher_term).astype(jnp.bfloat16), "feat").astype(
            jnp.float32
        )
        losses = losses + jnp.sum(differ * differ, axis=1)
        pulled = pulled + jnp.dot(
            differ.astype(jnp.bfloat16), other_unit, preferred_element_type=jnp.float32
        )
        return (losses, pulled)

    carry = (jnp.zeros((rows_here,), jnp.float32), jnp.zeros((rows_here, width), jnp.float32))
    carry = absorb(carry, packed)

    def turn(step, state):
        inner, visitor = state
        visitor = shifted(visitor, "rows", 1)
        return (absorb(inner, visitor), visitor)

    carry, visitor = lax.fori_loop(0, cycle - 1, turn, (carry, packed))
    losses, pulled = carry
    radial = lax.psum(jnp.sum(pulled * unit, axis=1), "feat")
    factor = 4.0 * D / embeds
    student_grad = factor * scaling[:, None] * (pulled - radial[:, None] * unit)
    return (D / embeds * losses, student_grad)


def solution(mesh):
    in_specs = (P(("groups", "rows"), "feat"), P(("groups", "rows"), "feat"))
    out_specs = (P(("groups", "rows")), P(("groups", "rows"), "feat"))
    return jax.shard_map(
        on_device, mesh=mesh, in_specs=in_specs, out_specs=out_specs, check_vma=False
    )
```

profile of v0, /device:TPU:0, one launch (start us, length us, event | category | flops | bytes accessed | tf_op | source)
XLA Modules:
  0.0 104.7 jit_solution(14661461870272374266)
XLA Ops:
  0.6 0.0 copy-start
  0.6 1.3 %multiply_reduce_fusion.2 = f32[160]{0:T(256)S(1)} fusion(f32[160,1024]{1,0:T(8,128)} %param.4), kind=kLoop, calls=%fused_computation.12 | loop fusion | flops 327520 | bytes 656000 | tf_op jit(solution)/shard_map/reduce_sum | solution.py:21
  1.9 8.3 %psum.28 = f32[160]{0:T(256)S(1)} all-reduce(f32[160]{0:T(256)S(1)} %multiply_reduce_fusion.2), channel_id=1, replica_groups=mesh['groups'=2,'rows'=4,'feat'=4] {'feat'}, use_global_device_ids=true, to_apply=%region_1.0 | all-reduce | flops 160 | bytes 1280 | tf_op jit(solution)/shard_map/psum | solution.py:21
  10.3 0.0 copy-done
  10.3 0.0 copy-start.1
  10.3 0.1 multiply_convert_fusion
  10.4 0.8 copy-done.1
  11.2 0.2 fusion.6
  11.3 0.3 fusion.5
  11.6 11.0 %psum.29 = bf16[160,160]{1,0:T(8,128)(2,1)S(1)} all-reduce(bf16[160,160]{1,0:T(8,128)(2,1)S(1)} %fusion.5), channel_id=1, replica_groups=mesh['groups'=2,'rows'=4,'feat'=4] {'feat'}, use_global_device_ids=true, to_apply=%region_2.0 | all-reduce | flops 25600 | bytes 102400 | tf_op jit(solution)/shard_map/psum | solution.py:38
  22.6 0.2 fusion.7
  22.8 0.1 multiply_reduce_fusion.3
  23.0 74.0 %while.14 = (s32[]{:T(128)}, f32[160]{0:T(256)S(1)}, f32[160,1024]{1,0:T(8,128)S(1)}, bf16[160,1280]{1,0:T(8,128)(2,1)S(1)}, bf16[160,1024]{1,0:T(8,128)(2,1)S(1)}, /*index=5*/bf16[160,256]{1,0:T(8,128)(2,1)S(1)}, s32[]{:T(128)}) while((s32[]{:T(128)}, f32[160]{0:T(256)S(1)}, f32[160,1024]{1,0:T(8,128)S(1)}, bf16[160,1280]{1,0:T(8,128)(2,1)S(1)}, ...), condition=%wide.region_7.0_spmd, body=%wide.region_4.0_spmd.sunk | while | flops 118282240 | bytes 5470837 | solution.py:55
  23.0 1.8 %collective-permute-start = (bf16[160,1280]{1,0:T(8,128)(2,1)S(1)}, bf16[160,1280]{1,0:T(8,128)(2,1)S(1)}, u32[]{:S(2)}, u32[]{:S(2)}) collective-permute-start(bf16[160,1280]{1,0:T(8,128)(2,1)S(1)} %get-tuple-element.98), channel_id=1, source_target_pairs={{12,0},{0,4},{4,8},{8,12},{13,1},{1,5},{5,9},{9,13},{14,2},{2,6},{... | collective-permute-start | bytes 1228808 | tf_op jit(solution)/shard_map/while/body/eval_jaxpr/ppermute | solution.py:13
  24.9 11.0 %collective-permute-done = bf16[160,1280]{1,0:T(8,128)(2,1)S(1)} collective-permute-done((bf16[160,1280]{1,0:T(8,128)(2,1)S(1)}, bf16[160,1280]{1,0:T(8,128)(2,1)S(1)}, u32[]{:S(2)}, u32[]{:S(2)}) %collective-permute-start) | collective-permute-done | bytes 409632 | tf_op jit(solution)/shard_map/while/body/eval_jaxpr/ppermute | solution.py:13
  35.9 0.2 fusion.31
  36.1 0.3 fusion.32
  36.3 11.0 %psum.32 = bf16[160,160]{1,0:T(8,128)(2,1)S(1)} all-reduce(bf16[160,160]{1,0:T(8,128)(2,1)S(1)} %fusion.32), channel_id=1, replica_groups=mesh['groups'=2,'rows'=4,'feat'=4] {'feat'}, use_global_device_ids=true, to_apply=%region_5.0 | all-reduce | flops 25600 | bytes 102400 | tf_op jit(solution)/shard_map/while/body/eval_jaxpr/psum | solution.py:38
  47.3 0.1 multiply_reduce_fusion.5
  47.5 0.2 convolution_add_fusion.2
  47.8 0.1 collective-permute-start
  47.8 12.7 %collective-permute-done = bf16[160,1280]{1,0:T(8,128)(2,1)S(1)} collective-permute-done((bf16[160,1280]{1,0:T(8,128)(2,1)S(1)}, bf16[160,1280]{1,0:T(8,128)(2,1)S(1)}, u32[]{:S(2)}, u32[]{:S(2)}) %collective-permute-start) | collective-permute-done | bytes 409632 | tf_op jit(solution)/shard_map/while/body/eval_jaxpr/ppermute | solution.py:13
  60.5 0.2 fusion.31
  60.7 0.3 fusion.32
  61.0 10.9 %psum.32 = bf16[160,160]{1,0:T(8,128)(2,1)S(1)} all-reduce(bf16[160,160]{1,0:T(8,128)(2,1)S(1)} %fusion.32), channel_id=1, replica_groups=mesh['groups'=2,'rows'=4,'feat'=4] {'feat'}, use_global_device_ids=true, to_apply=%region_5.0 | all-reduce | flops 25600 | bytes 102400 | tf_op jit(solution)/shard_map/while/body/eval_jaxpr/psum | solution.py:38
  71.9 0.1 multiply_reduce_fusion.5
  72.1 0.2 convolution_add_fusion.2
  72.3 0.1 collective-permute-start
  72.4 12.8 %collective-permute-done = bf16[160,1280]{1,0:T(8,128)(2,1)S(1)} collective-permute-done((bf16[160,1280]{1,0:T(8,128)(2,1)S(1)}, bf16[160,1280]{1,0:T(8,128)(2,1)S(1)}, u32[]{:S(2)}, u32[]{:S(2)}) %collective-permute-start) | collective-permute-done | bytes 409632 | tf_op jit(solution)/shard_map/while/body/eval_jaxpr/ppermute | solution.py:13
  85.2 0.2 fusion.31
  85.4 0.3 fusion.32
  85.7 10.9 %psum.32 = bf16[160,160]{1,0:T(8,128)(2,1)S(1)} all-reduce(bf16[160,160]{1,0:T(8,128)(2,1)S(1)} %fusion.32), channel_id=1, replica_groups=mesh['groups'=2,'rows'=4,'feat'=4] {'feat'}, use_global_device_ids=true, to_apply=%region_5.0 | all-reduce | flops 25600 | bytes 102400 | tf_op jit(solution)/shard_map/while/body/eval_jaxpr/psum | solution.py:38
  96.6 0.1 multiply_reduce_fusion.5
  96.7 0.2 convolution_add_fusion.2
  97.0 0.2 multiply_reduce_fusion.1
  97.2 5.9 %psum.30 = f32[160]{0:T(256)S(1)} all-reduce(f32[160]{0:T(256)S(1)} %multiply_reduce_fusion.1), channel_id=1, replica_groups=mesh['groups'=2,'rows'=4,'feat'=4] {'feat'}, use_global_device_ids=true, to_apply=%region_9.0 | all-reduce | flops 160 | bytes 1280 | tf_op jit(solution)/shard_map/psum | solution.py:57
  103.1 1.0 subtract_multiply_fusion
  104.1 0.6 broadcast_multiply_fusion.1
  (8 shorter events, 0.2 us)
Async XLA Ops:
  0.6 9.6 %copy-start = (f32[160,1024]{1,0:T(8,128)S(1)}, f32[160,1024]{1,0:T(8,128)}, u32[]{:S(2)}) copy-start(f32[160,1024]{1,0:T(8,128)} %param.4) | copy-start | bytes 1966084
  10.3 0.9 copy-start.1
  23.0 12.9 %collective-permute-start = (bf16[160,1280]{1,0:T(8,128)(2,1)S(1)}, bf16[160,1280]{1,0:T(8,128)(2,1)S(1)}, u32[]{:S(2)}, u32[]{:S(2)}) collective-permute-start(bf16[160,1280]{1,0:T(8,128)(2,1)S(1)} %get-tuple-element.98), channel_id=1, source_target_pairs={{12,0},{0,4},{4,8},{8,12},{13,1},{1,5},{5,9},{9,13},{14,2},{2,6},{... | collective-permute-start | bytes 1228808 | tf_op jit(solution)/shard_map/while/body/eval_jaxpr/ppermute | solution.py:13
  47.8 12.8 %collective-permute-start = (bf16[160,1280]{1,0:T(8,128)(2,1)S(1)}, bf16[160,1280]{1,0:T(8,128)(2,1)S(1)}, u32[]{:S(2)}, u32[]{:S(2)}) collective-permute-start(bf16[160,1280]{1,0:T(8,128)(2,1)S(1)} %get-tuple-element.98), channel_id=1, source_target_pairs={{12,0},{0,4},{4,8},{8,12},{13,1},{1,5},{5,9},{9,13},{14,2},{2,6},{... | collective-permute-start | bytes 1228808 | tf_op jit(solution)/shard_map/while/body/eval_jaxpr/ppermute | solution.py:13
  72.3 12.9 %collective-permute-start = (bf16[160,1280]{1,0:T(8,128)(2,1)S(1)}, bf16[160,1280]{1,0:T(8,128)(2,1)S(1)}, u32[]{:S(2)}, u32[]{:S(2)}) collective-permute-start(bf16[160,1280]{1,0:T(8,128)(2,1)S(1)} %get-tuple-element.98), channel_id=1, source_target_pairs={{12,0},{0,4},{4,8},{8,12},{13,1},{1,5},{5,9},{9,13},{14,2},{2,6},{... | collective-permute-start | bytes 1228808 | tf_op jit(solution)/shard_map/while/body/eval_jaxpr/ppermute | solution.py:13
where the time goes:
time: 105 us
  blocking collectives  58.1 us (55%)
  waiting for transfers between devices  36.5 us (35%)
  other arithmetic  3.7 us (4%)
  matrix products  2.71 us (3%)
  starting transfers between devices  1.96 us (2%)
    psum x4, blocking collectives, absorb(): lax.psum((student_term - teacher_term).astype(jnp.bfloat16), 'feat')  43.8 us
    ppermute x3, waiting for transfers between devices, shifted(): return lax.ppermute(block, axis, route)  36.5 us
    psum x1, blocking collectives, on_device(): squares = lax.psum(jnp.sum(student * student, axis=1), 'feat')  8.34 us
    psum x1, blocking collectives, on_device(): radial = lax.psum(jnp.sum(pulled * unit, axis=1), 'feat')  5.89 us
  transfers between devices with their start and end apart: 3, of which 3 were waited for; matrix products, arithmetic and copies ran while one was open for 0% of the time, Pallas kernels for 0%

commit v1 on v0

--- a/solution.py
+++ b/solution.py
@@ -18,7 +18,8 @@
     rows_here = student.shape[0]
     width = student.shape[1]
     embeds = rows_here * cycle
-    squares = lax.psum(jnp.sum(student * student, axis=1), "feat")
+    obj = jnp.sum(student * student, axis=1)
+    squares = jnp.sum(lax.all_gather(obj, axis_name="feat"), 0)
     scaling = lax.rsqrt(squares + EPSILON)
     unit = student * scaling[:, None]
     unit_half = unit.astype(jnp.bfloat16)

time: 105 us -> 107 us (1.019)
  local copies, waits for them, and re-layouts: 0.87 us -> 2.41 us
    psum x1 -> x0, blocking collectives: 8.34 us -> none  [on_device(): squares = lax.psum(jnp.sum(student * student, axis=1), 'feat')]
    unnamed x0 -> x1, blocking collectives: none -> 8.31 us
    unnamed x4 -> x9, local copies, waits for them, and re-layouts: 0.78 us -> 2.24 us
where the time goes in v1:
time: 107 us
  blocking collectives  58.1 us (54%)
  waiting for transfers between devices  36.5 us (34%)
  other arithmetic  3.66 us (3%)
  matrix products  2.71 us (3%)
  local copies, waits for them, and re-layouts  2.41 us (2%)
  starting transfers between devices  1.96 us (2%)
  between operations  1.39 us (1%)
    psum x4, blocking collectives, absorb(): lax.psum((student_term - teacher_term).astype(jnp.bfloat16), 'feat')  43.9 us
    ppermute x3, waiting for transfers between devices, shifted(): return lax.ppermute(block, axis, route)  36.5 us
    unnamed x1, blocking collectives  8.31 us
    psum x1, blocking collectives, on_device(): radial = lax.psum(jnp.sum(pulled * unit, axis=1), 'feat')  5.91 us
    unnamed x9, local copies, waits for them, and re-layouts  2.24 us
  transfers between devices with their start and end apart: 3, of which 3 were waited for; matrix products, arithmetic and copies ran while one was open for 0% of the time, Pallas kernels for 0%

profile of v1, /device:TPU:0, one launch (start us, length us, event | category | flops | bytes accessed | tf_op | source)
XLA Modules:
  0.0 106.9 jit_solution(12869327582182654565)
XLA Ops:
  0.6 0.0 copy-start.2
  0.6 0.0 copy-start
  0.7 0.6 copy-done.2
  1.3 0.6 dynamic-slice
  2.5 1.2 %multiply_reduce_fusion.2 = f32[160]{0:T(256)S(1)} fusion(f32[160,1024]{1,0:T(8,128)} %param.4), kind=kLoop, calls=%fused_computation.12 | loop fusion | flops 327520 | bytes 656000 | tf_op jit(solution)/shard_map/reduce_sum | solution.py:21
  3.7 0.2 dynamic-update-slice
  4.0 8.3 %all-reduce = f32[640]{0:T(1024)S(1)} all-reduce(f32[640]{0:T(1024)S(1)} %dynamic-update-slice), channel_id=2, replica_groups=mesh['groups'=2,'rows'=4,'feat'=4] {'feat'}, use_global_device_ids=true, to_apply=%add | all-reduce | flops 640 | bytes 5120
  12.3 0.1 reshape.13
  12.4 0.0 copy-done
  12.4 0.0 copy-start.1
  12.4 0.1 multiply_convert_fusion
  12.6 0.8 copy-done.1
  13.3 0.2 fusion.6
  13.5 0.3 fusion.5
  13.8 11.0 %psum.21 = bf16[160,160]{1,0:T(8,128)(2,1)S(1)} all-reduce(bf16[160,160]{1,0:T(8,128)(2,1)S(1)} %fusion.5), channel_id=1, replica_groups=mesh['groups'=2,'rows'=4,'feat'=4] {'feat'}, use_global_device_ids=true, to_apply=%region_2.0 | all-reduce | flops 25600 | bytes 102400 | tf_op jit(solution)/shard_map/psum | solution.py:39
  24.8 0.2 fusion.7
  25.0 0.1 multiply_reduce_fusion.3
  25.2 74.0 %while.14 = (s32[]{:T(128)}, f32[160]{0:T(256)S(1)}, f32[160,1024]{1,0:T(8,128)S(1)}, bf16[160,1280]{1,0:T(8,128)(2,1)S(1)}, bf16[160,1024]{1,0:T(8,128)(2,1)S(1)}, /*index=5*/bf16[160,256]{1,0:T(8,128)(2,1)S(1)}, s32[]{:T(128)}) while((s32[]{:T(128)}, f32[160]{0:T(256)S(1)}, f32[160,1024]{1,0:T(8,128)S(1)}, bf16[160,1280]{1,0:T(8,128)(2,1)S(1)}, ...), condition=%wide.region_7.0_spmd, body=%wide.region_4.0_spmd.sunk | while | flops 118282240 | bytes 5470837 | solution.py:56
  25.2 1.8 %collective-permute-start = (bf16[160,1280]{1,0:T(8,128)(2,1)S(1)}, bf16[160,1280]{1,0:T(8,128)(2,1)S(1)}, u32[]{:S(2)}, u32[]{:S(2)}) collective-permute-start(bf16[160,1280]{1,0:T(8,128)(2,1)S(1)} %get-tuple-element.98), channel_id=1, source_target_pairs={{12,0},{0,4},{4,8},{8,12},{13,1},{1,5},{5,9},{9,13},{14,2},{2,6},{... | collective-permute-start | bytes 1228808 | tf_op jit(solution)/shard_map/while/body/eval_jaxpr/ppermute | solution.py:13
  27.0 11.0 %collective-permute-done = bf16[160,1280]{1,0:T(8,128)(2,1)S(1)} collective-permute-done((bf16[160,1280]{1,0:T(8,128)(2,1)S(1)}, bf16[160,1280]{1,0:T(8,128)(2,1)S(1)}, u32[]{:S(2)}, u32[]{:S(2)}) %collective-permute-start) | collective-permute-done | bytes 409632 | tf_op jit(solution)/shard_map/while/body/eval_jaxpr/ppermute | solution.py:13
  38.0 0.2 fusion.31
  38.2 0.3 fusion.32
  38.5 11.0 %psum.24 = bf16[160,160]{1,0:T(8,128)(2,1)S(1)} all-reduce(bf16[160,160]{1,0:T(8,128)(2,1)S(1)} %fusion.32), channel_id=1, replica_groups=mesh['groups'=2,'rows'=4,'feat'=4] {'feat'}, use_global_device_ids=true, to_apply=%region_5.0 | all-reduce | flops 25600 | bytes 102400 | tf_op jit(solution)/shard_map/while/body/eval_jaxpr/psum | solution.py:39
  49.5 0.1 multiply_reduce_fusion.5
  49.7 0.2 convolution_add_fusion.2
  50.0 0.1 collective-permute-start
  50.0 12.7 %collective-permute-done = bf16[160,1280]{1,0:T(8,128)(2,1)S(1)} collective-permute-done((bf16[160,1280]{1,0:T(8,128)(2,1)S(1)}, bf16[160,1280]{1,0:T(8,128)(2,1)S(1)}, u32[]{:S(2)}, u32[]{:S(2)}) %collective-permute-start) | collective-permute-done | bytes 409632 | tf_op jit(solution)/shard_map/while/body/eval_jaxpr/ppermute | solution.py:13
  62.7 0.2 fusion.31
  62.9 0.3 fusion.32
  63.1 10.9 %psum.24 = bf16[160,160]{1,0:T(8,128)(2,1)S(1)} all-reduce(bf16[160,160]{1,0:T(8,128)(2,1)S(1)} %fusion.32), channel_id=1, replica_groups=mesh['groups'=2,'rows'=4,'feat'=4] {'feat'}, use_global_device_ids=true, to_apply=%region_5.0 | all-reduce | flops 25600 | bytes 102400 | tf_op jit(solution)/shard_map/while/body/eval_jaxpr/psum | solution.py:39
  74.1 0.1 multiply_reduce_fusion.5
  74.2 0.2 convolution_add_fusion.2
  74.5 0.1 collective-permute-start
  74.6 12.8 %collective-permute-done = bf16[160,1280]{1,0:T(8,128)(2,1)S(1)} collective-permute-done((bf16[160,1280]{1,0:T(8,128)(2,1)S(1)}, bf16[160,1280]{1,0:T(8,128)(2,1)S(1)}, u32[]{:S(2)}, u32[]{:S(2)}) %collective-permute-start) | collective-permute-done | bytes 409632 | tf_op jit(solution)/shard_map/while/body/eval_jaxpr/ppermute | solution.py:13
  87.3 0.2 fusion.31
  87.5 0.3 fusion.32
  87.8 10.9 %psum.24 = bf16[160,160]{1,0:T(8,128)(2,1)S(1)} all-reduce(bf16[160,160]{1,0:T(8,128)(2,1)S(1)} %fusion.32), channel_id=1, replica_groups=mesh['groups'=2,'rows'=4,'feat'=4] {'feat'}, use_global_device_ids=true, to_apply=%region_5.0 | all-reduce | flops 25600 | bytes 102400 | tf_op jit(solution)/shard_map/while/body/eval_jaxpr/psum | solution.py:39
  98.7 0.1 multiply_reduce_fusion.5
  98.9 0.2 convolution_add_fusion.2
  99.1 0.2 multiply_reduce_fusion.1
  99.4 5.9 %psum.22 = f32[160]{0:T(256)S(1)} all-reduce(f32[160]{0:T(256)S(1)} %multiply_reduce_fusion.1), channel_id=1, replica_groups=mesh['groups'=2,'rows'=4,'feat'=4] {'feat'}, use_global_device_ids=true, to_apply=%region_9.0 | all-reduce | flops 160 | bytes 1280 | tf_op jit(solution)/shard_map/psum | solution.py:58
  105.3 1.0 subtract_multiply_fusion
  106.3 0.6 broadcast_multiply_fusion.1
  (10 shorter events, 0.2 us)
Async XLA Ops:
  0.6 0.7 copy-start.2
  0.6 11.8 %copy-start = (f32[160,1024]{1,0:T(8,128)S(1)}, f32[160,1024]{1,0:T(8,128)}, u32[]{:S(2)}) copy-start(f32[160,1024]{1,0:T(8,128)} %param.4) | copy-start | bytes 1966084
  12.4 0.9 copy-start.1
  25.2 12.8 %collective-permute-start = (bf16[160,1280]{1,0:T(8,128)(2,1)S(1)}, bf16[160,1280]{1,0:T(8,128)(2,1)S(1)}, u32[]{:S(2)}, u32[]{:S(2)}) collective-permute-start(bf16[160,1280]{1,0:T(8,128)(2,1)S(1)} %get-tuple-element.98), channel_id=1, source_target_pairs={{12,0},{0,4},{4,8},{8,12},{13,1},{1,5},{5,9},{9,13},{14,2},{2,6},{... | collective-permute-start | bytes 1228808 | tf_op jit(solution)/shard_map/while/body/eval_jaxpr/ppermute | solution.py:13
  50.0 12.7 %collective-permute-start = (bf16[160,1280]{1,0:T(8,128)(2,1)S(1)}, bf16[160,1280]{1,0:T(8,128)(2,1)S(1)}, u32[]{:S(2)}, u32[]{:S(2)}) collective-permute-start(bf16[160,1280]{1,0:T(8,128)(2,1)S(1)} %get-tuple-element.98), channel_id=1, source_target_pairs={{12,0},{0,4},{4,8},{8,12},{13,1},{1,5},{5,9},{9,13},{14,2},{2,6},{... | collective-permute-start | bytes 1228808 | tf_op jit(solution)/shard_map/while/body/eval_jaxpr/ppermute | solution.py:13
  74.5 12.9 %collective-permute-start = (bf16[160,1280]{1,0:T(8,128)(2,1)S(1)}, bf16[160,1280]{1,0:T(8,128)(2,1)S(1)}, u32[]{:S(2)}, u32[]{:S(2)}) collective-permute-start(bf16[160,1280]{1,0:T(8,128)(2,1)S(1)} %get-tuple-element.98), channel_id=1, source_target_pairs={{12,0},{0,4},{4,8},{8,12},{13,1},{1,5},{5,9},{9,13},{14,2},{2,6},{... | collective-permute-start | bytes 1228808 | tf_op jit(solution)/shard_map/while/body/eval_jaxpr/ppermute | solution.py:13
